TPU v7x, 128 devices: a whole 4x4x4 slice. The times are simulated.
128 devices in a mesh: tm: 32 (over y, z_hi, x), head: 4 (over z_lo, core).
Axes of the slice: x: 4, y: 4, z: 4 (z_hi: 2, z_lo: 2; z = z_hi * 2 + z_lo), core: 2. Of those that a mesh axis runs over, the one named last changes fastest.
Arguments:
- frames: bfloat16 [64, 512, 5120], P('tm', None, 'head'), may hold values from -8 to 8
- taps: float32 [3, 5120], P(None, 'head'), may hold values from -3 to 3
- w_query: bfloat16 [5120, 2560], P(None, 'head')
- w_key: bfloat16 [5120, 2560], P(None, 'head')
- w_value: bfloat16 [5120, 2560], P(None, 'head'), may hold values from -0.078125 to 0.078125
- q_gain: float32 [2560], P('head'), may hold values from 0.5 to 6
- k_gain: float32 [2560], P('head'), may hold values from 0.5 to 6
Outputs:
- attended: bfloat16 [64, 512, 2560], P('tm', None, 'head')
All inputs are finite; a program needn't handle non-finite values.
Results may differ from a plain program's by a relative error of at most 0.0086.
Values may be sent and summed in bfloat16 or wider, within the bound.
A program may use at most 192 MiB of HBM per device.

v0:
```python
import jax
import jax.numpy as jnp
from jax import lax
from jax.sharding import PartitionSpec as P

DH = 128


def padded_2(x, sides, width):
    for axis, dim in sides:
        count, length = (lax.axis_size(axis), x.shape[dim])
        up = [(i, (i + 1) % count) for i in range(count - 1)]
        down = [(j, i) for i, j in up]
        last = lax.slice_in_dim(x, length - width, length, axis=dim)
        initial = lax.slice_in_dim(x, 0, width, axis=dim)
        before = lax.ppermute(last, axis, up)
        after = lax.ppermute(initial, axis, down)
        x = jnp.concatenate([before, x, after], axis=dim)
    return x


def shifted(value, axis, steps):
    count = lax.axis_size(axis)
    initial, last = (max(0, -steps), min(count, count - steps))
    return lax.ppermute(value, axis, [(source, source + steps) for source in range(initial, last)])


def broadcast(x, axis, root):
    mine = lax.axis_index(axis) == root
    return lax.psum(jnp.where(mine, x, jnp.zeros_like(x)), axis)


def convolve(padded, taps, first, count):
    centre = padded[first : first + count].astype(jnp.float32)
    before = padded[first - 1 : first - 1 + count].astype(jnp.float32)
    after = padded[first + 1 : first + 1 + count].astype(jnp.float32)
    return (centre + taps[0] * before + taps[1] * centre + taps[2] * after).astype(jnp.bfloat16)


def normalize(projected, gain):
    heads_dev = projected.shape[1] // DH
    split_heads = projected.reshape(projected.shape[0], heads_dev, DH)
    mean_sq = jnp.mean(split_heads * split_heads, axis=-1, keepdims=True)
    scaled = split_heads * lax.rsqrt(mean_sq + 1e-06)
    return scaled.reshape(projected.shape[0], heads_dev * DH) * gain


def per_device(frames, taps, w_query, w_key, w_value, q_gain, k_gain):
    frame_dev = frames.shape[0]
    tok_count = frames.shape[1]
    padded = padded_2(frames, (("tm", 0),), 1)
    mixed = convolve(padded, taps, 1, frame_dev)
    frame_count = mixed.shape[0]
    tok_rows = mixed.reshape(frame_count * tok_count, mixed.shape[2])
    col_count = w_query.shape[1]
    heads_dev = col_count // DH
    piece = lax.all_gather(tok_rows, "head", axis=1, tiled=True)
    q_part = jnp.dot(piece, w_query, preferred_element_type=jnp.float32)
    k_part = jnp.dot(piece, w_key, preferred_element_type=jnp.float32)
    v_part = jnp.dot(piece, w_value, preferred_element_type=jnp.float32)
    query = (
        normalize(q_part, q_gain)
        .astype(jnp.bfloat16)
        .reshape(frame_count, tok_count, heads_dev, DH)
    )
    key_proj = (
        normalize(k_part, k_gain)
        .astype(jnp.bfloat16)
        .reshape(frame_count, tok_count, heads_dev, DH)
    )
    value_proj = v_part.astype(jnp.bfloat16).reshape(frame_count, tok_count, heads_dev, DH)
    stacked = jnp.stack([key_proj, value_proj], axis=1)
    at_start = lax.axis_index("tm") == 0
    received = shifted(stacked[-1], "tm", 1)
    previous = jnp.where(at_start, stacked[0], received)
    anchor = broadcast(stacked[0], "tm", 0)
    predecessors = jnp.concatenate([previous[None], stacked[:-1]], axis=0)
    anchors = jnp.broadcast_to(anchor[None], predecessors.shape)
    context = jnp.concatenate([anchors, predecessors], axis=2)
    scale = 1.0 / DH**0.5
    scores = (
        jnp.einsum("fqhd,fkhd->fhqk", query, context[:, 0], preferred_element_type=jnp.float32)
        * scale
    )
    top = jnp.max(scores, axis=-1, keepdims=True)
    expo = jnp.exp(scores - top)
    probs = (expo / jnp.sum(expo, axis=-1, keepdims=True)).astype(jnp.bfloat16)
    result = jnp.einsum("fhqk,fkhd->fqhd", probs, context[:, 1], preferred_element_type=jnp.float32)
    return result.astype(jnp.bfloat16).reshape(frame_dev, tok_count, heads_dev * DH)


def solution(mesh):
    placed = (
        P("tm", None, "head"),
        P(None, "head"),
        P(None, "head"),
        P(None, "head"),
        P(None, "head"),
        P("head"),
        P("head"),
    )
    return jax.shard_map(
        per_device, mesh=mesh, in_specs=placed, out_specs=P("tm", None, "head"), check_vma=False
    )
```

profile of v0, /device:TPU:0, one launch (start us, length us, event | category | flops | bytes accessed | tf_op | source)
XLA Modules:
  0.0 618.8 jit_solution(13300280968242198821)
XLA Ops:
  6.5 2.0 fusion.26
  8.6 3.6 collective-permute-start
  12.2 1.3 collective-permute-start.1
  13.5 26.6 %collective-permute-done = bf16[1,512,1280]{2,1,0:T(8,128)(2,1)S(1)} collective-permute-done((bf16[1,512,1280]{2,1,0:T(8,128)(2,1)S(1)}, bf16[1,512,1280]{2,1,0:T(8,128)(2,1)S(1)}, u32[]{:S(2)}, u32[]{:S(2)}) %collective-permute-start) | collective-permute-done | bytes 1310752 | tf_op jit(solution)/shard_map/ppermute | solution.py:16
  40.1 4.2 collective-permute-done.1
  44.3 2.8 fusion.10
  47.1 0.0 all-gather.2.cloned.1.call-update
  47.1 0.0 all-reduce.2.cloned.1.call-start
  47.2 103.5 %all-gather.2.cloned.1.call-done = bf16[1024,5120]{1,0:T(8,128)(2,1)} async-done(((bf16[1024,1280]{1,0:T(8,128)(2,1)}), bf16[1024,5120]{1,0:T(8,128)(2,1)}) %all-gather.2.cloned.1.call-update) | async-done | bytes 10485776 | tf_op jit(solution)/shard_map/all_gather | solution.py:57
  150.7 12.9 %convolution_convert_fusion = bf16[1024,640]{1,0:T(8,128)(2,1)S(1)} fusion(bf16[1024,5120]{1,0:T(8,128)(2,1)} %all-gather.2.cloned.1.call-done, bf16[5120,640]{1,0:T(8,128)(2,1)} %param.11), kind=kOutput, calls=%fused_computation.28 | convolution fusion | flops 6711541760 | bytes 18350080 | tf_op jit(solution)/shard_map/dot_general | solution.py:60
  163.6 1.5 reshape.44
  165.1 0.2 copy.17
  165.3 13.1 %fusion.27 = (f32[1024,640]{0,1:T(8,128)}, f32[1024,640]{0,1:T(8,128)}) fusion(bf16[1024,5120]{1,0:T(8,128)(2,1)} %all-gather.2.cloned.1.call-done, bf16[5120,640]{1,0:T(8,128)(2,1)} %param.10), kind=kOutput, calls=%fused_computation.45 | convolution fusion | flops 6711541760 | bytes 22282240 | tf_op jit(solution)/shard_map/dot_general | solution.py:59
  178.5 2.0 reduce_sum.27
  180.5 2.0 fusion.14
  182.5 1.8 stack_reshape.6
  184.3 3.5 copy.16
  187.8 1.7 fusion.18
  189.5 4.4 collective-permute-start.2
  194.0 27.4 %collective-permute-done.2 = bf16[2,512,5,128]{3,1,2,0:T(8,128)(2,1)} collective-permute-done((bf16[2,512,5,128]{3,1,2,0:T(8,128)(2,1)}, bf16[2,512,5,128]{3,1,2,0:T(8,128)(2,1)}, u32[]{:S(2)}, u32[]{:S(2)}) %collective-permute-start.2) | collective-permute-done | bytes 1310752 | tf_op jit(solution)/shard_map/ppermute | solution.py:25
  221.4 1.7 bitcast_select_fusion.1
  223.1 12.7 %fusion.28 = (f32[1024,640]{0,1:T(8,128)S(1)}, f32[1024,640]{0,1:T(8,128)}) fusion(bf16[1024,5120]{1,0:T(8,128)(2,1)} %all-gather.2.cloned.1.call-done, bf16[5120,640]{1,0:T(8,128)(2,1)} %param.9), kind=kOutput, calls=%fused_computation.46 | convolution fusion | flops 6711541760 | bytes 22282240 | tf_op jit(solution)/shard_map/dot_general | solution.py:58
  235.8 0.2 reduce_sum.28
  236.1 0.4 copy-done.5
  236.5 2.0 fusion.12
  238.6 1.8 reshape.42
  240.4 343.4 %all-reduce.2.cloned.1.call-done = bf16[2,512,5,128]{3,1,2,0:T(8,128)(2,1)} async-done(((bf16[2,512,5,128]{3,1,2,0:T(8,128)(2,1)}), bf16[2,512,5,128]{3,1,2,0:T(8,128)(2,1)}) %all-reduce.2.cloned.1.call-update) | async-done | bytes 1310736 | tf_op jit(solution)/shard_map/psum | solution.py:30
  583.8 1.8 broadcast_in_dim.7
  585.7 2.7 maximum_maximum_fusion
  588.4 12.6 %fusion.29 = (f32[2,5,512]{2,1,0:T(8,128)S(1)}, f32[2,5,512,1024]{3,2,1,0:T(8,128)}) fusion(bf16[2,2,1024,5,128]{4,2,3,0,1:T(8,128)(2,1)} %maximum_maximum_fusion, bf16[2,512,5,128]{1,0,3,2:T(2,128)(2,1)} %reshape.42), kind=kOutput, calls=%fused_computation.47 | convolution fusion | flops 1357906944 | bytes 24924160 | tf_op jit(solution)/shard_map/sub | solution.py:86
  601.0 9.5 %fusion.16 = bf16[2,5,128,512]{3,2,1,0:T(8,128)(2,1)S(1)} fusion(f32[2,5,512,1024]{3,2,1,0:T(8,128)} %get-tuple-element.19, f32[2,5,512]{2,1,0:T(8,128)S(1)} %get-tuple-element.18, bf16[2,2,1024,5,128]{4,2,3,0,1:T(8,128)(2,1)} %maximum_maximum_fusion), kind=kOutput, calls=%fused_computation.27 | convolution fusion | flops 1353318400 | bytes 24924160 | tf_op jit(solution)/shard_map/fhqk,fkhd->fqhd/dot_general | solution.py:88
  610.5 1.4 copy.22
  (16 shorter events, 0.1 us)
Async XLA Ops:
  6.5 37.8 %copy-start = (bf16[2,512,1280]{2,1,0:T(8,128)(2,1)S(1)}, bf16[2,512,1280]{2,1,0:T(8,128)(2,1)}, u32[]{:S(2)}) copy-start(bf16[2,512,1280]{2,1,0:T(8,128)(2,1)} %param.7) | copy-start | bytes 7864324
  6.5 6.9 %copy-start.3 = (f32[3,1280]{1,0:T(4,128)S(1)}, f32[3,1280]{1,0:T(4,128)}, u32[]{:S(2)}) copy-start(f32[3,1280]{1,0:T(4,128)} %param.8) | copy-start | bytes 46084
  6.5 144.2 %all-gather.2.cloned.1.call-start = ((), (), s32[]{:S(2)}) async-start(), calls=%async_computation | async-start | bytes 13107200 | tf_op jit(solution)/shard_map/all_gather | solution.py:57
  8.6 31.5 %collective-permute-start = (bf16[1,512,1280]{2,1,0:T(8,128)(2,1)S(1)}, bf16[1,512,1280]{2,1,0:T(8,128)(2,1)S(1)}, u32[]{:S(2)}, u32[]{:S(2)}) collective-permute-start(bf16[1,512,1280]{2,1,0:T(8,128)(2,1)S(1)} %get-tuple-element.12), channel_id=1, source_target_pairs={{0,4},{4,8},{8,12},{12,16},{16,20},{20,24},{24,28},{28,32},{32,36}... | collective-permute-start | bytes 3932168 | tf_op jit(solution)/shard_map/ppermute | solution.py:16
  12.2 32.1 %collective-permute-start.1 = (bf16[1,512,1280]{2,1,0:T(8,128)(2,1)S(1)}, bf16[1,512,1280]{2,1,0:T(8,128)(2,1)S(1)}, u32[]{:S(2)}, u32[]{:S(2)}) collective-permute-start(bf16[1,512,1280]{2,1,0:T(8,128)(2,1)S(1)} %get-tuple-element.13), channel_id=1, source_target_pairs={{4,0},{8,4},{12,8},{16,12},{20,16},{24,20},{28,24},{32,28},{36,32}... | collective-permute-start | bytes 3932168 | tf_op jit(solution)/shard_map/ppermute | solution.py:17
  47.1 536.7 %all-reduce.2.cloned.1.call-start = ((), (), s32[]{:S(2)}) async-start(), calls=%async_computation.1 | async-start | bytes 2621440 | tf_op jit(solution)/shard_map/psum | solution.py:30
  178.5 2.0 copy-start.4
  189.5 31.8 %collective-permute-start.2 = (bf16[2,512,5,128]{3,1,2,0:T(8,128)(2,1)}, bf16[2,512,5,128]{3,1,2,0:T(8,128)(2,1)}, u32[]{:S(2)}, u32[]{:S(2)}) collective-permute-start(bf16[2,512,5,128]{3,1,2,0:T(8,128)(2,1)} %get-tuple-element.10), channel_id=1, source_target_pairs={{0,4},{4,8},{8,12},{12,16},{16,20},{20,24},{24,28},{28,32},{32,36}... | collective-permute-start | bytes 3932168 | tf_op jit(solution)/shard_map/ppermute | solution.py:25
  235.8 0.7 copy-start.5
  240.4 345.3 %copy-start.1 = (bf16[1,2,512,5,128]{4,2,3,0,1:T(8,128)(2,1)S(1)}, bf16[1,2,512,5,128]{4,2,3,0,1:T(8,128)(2,1)}, u32[]{:S(2)}) copy-start(bf16[1,2,512,5,128]{4,2,3,0,1:T(8,128)(2,1)} %get-tuple-element.11) | copy-start | bytes 3932164
  240.4 345.3 %copy-start.2 = (bf16[1,2,512,5,128]{4,2,3,0,1:T(8,128)(2,1)S(1)}, bf16[1,2,512,5,128]{4,2,3,0,1:T(8,128)(2,1)}, u32[]{:S(2)}) copy-start(bf16[1,2,512,5,128]{4,2,3,0,1:T(8,128)(2,1)} %get-tuple-element.9) | copy-start | bytes 3932164
Sparse Core Ops, SparseCore 0:
  47.2 103.4 all-gather.1
  223.2 360.5 all-reduce.1
where the time goes:
time: 619 us
  waiting for transfers between devices  505 us (82%)
  matrix products  60.9 us (10%)
  other arithmetic  15.2 us (2%)
  local copies, waits for them, and re-layouts  14.7 us (2%)
  between operations  13.5 us (2%)
  starting transfers between devices  9.37 us (2%)
    psum x1, waiting for transfers between devices, broadcast(): return lax.psum(jnp.where(mine, x, jnp.zeros_like(x)), axis)  343 us
    all_gather x1, waiting for transfers between devices, per_device(): piece = lax.all_gather(tok_rows, 'head', axis=1, tiled=True)  104 us
    ppermute x1, waiting for transfers between devices, shifted(): lax.ppermute(value, axis, [(source, source + steps) for source in range(i...  27.4 us
    ppermute x1, waiting for transfers between devices, padded_2(): before = lax.ppermute(last, axis, up)  26.6 us
    dot_general x1, matrix products, per_device(): k_part = jnp.dot(piece, w_key, preferred_element_type=jnp.float32)  13.1 us
    dot_general x1, matrix products, per_device(): v_part = jnp.dot(piece, w_value, preferred_element_type=jnp.float32)  12.9 us
    dot_general x1, matrix products, per_device(): q_part = jnp.dot(piece, w_query, preferred_element_type=jnp.float32)  12.7 us
    sub x1, matrix products, per_device(): expo = jnp.exp(scores - top)  12.6 us
  transfers between devices with their start and end apart: 5, of which 5 were waited for; matrix products, arithmetic and copies ran while one was open for 3% of the time, Pallas kernels for 0%

commit v1 on v0

v1 whole, which is shorter than its diff:
```python
import functools
import math

import jax
import jax.numpy as jnp
from jax import lax
from jax.experimental import pallas as pl
from jax.experimental.pallas import tpu as pltpu
from jax.sharding import PartitionSpec as P

DH = 128
MESH = pl.DeviceIdType.MESH
F32 = jnp.float32
BF16 = jnp.bfloat16

NX = 4
ROW = 2 * NX
PIECES = 16
STEP = 128
GROUP = 256


def kernel(frames, taps, gain_kv, gain_q, wq, wk, wv, out, XF, M, W, KVB, Q,
           w_sem, f_sem, hs, hr, zs, zr, cs, cr, fs, fr, ks, kr, ls, bs, pr):
    n_tm = lax.axis_size("tm")
    t = lax.axis_index("tm")
    h = lax.axis_index("head")
    tok = frames.shape[1]
    ch = frames.shape[2]
    cols = wq.shape[1]
    heads = cols // DH
    chunks = tok // STEP
    halves = tok // GROUP
    piece_rows = tok // PIECES

    is_first = t == 0
    is_last = t == n_tm - 1
    x_pos = lax.rem(t, NX)
    z_hi = lax.rem(t // NX, 2)
    pos = (t // ROW) * NX + x_pos
    up = lax.rem(t + 1, n_tm)
    down = lax.rem(t + n_tm - 1, n_tm)
    z_slot = lax.rem(h + 2, 4)
    c_slot = h + 1 - 2 * lax.rem(h, 2)
    f_slot = lax.rem(c_slot + 2, 4)
    other = t + NX - 2 * NX * z_hi

    def member(j, plane):
        return (j // NX) * ROW + plane * NX + lax.rem(j, NX)

    def frame_load(c):
        rows = pl.ds(pl.multiple_of(c * STEP, STEP), STEP)
        return pltpu.make_async_copy(frames.at[:, rows, :], XF.at[pl.ds(1, 2), rows, :], f_sem.at[c])

    for c in range(chunks):
        frame_load(c).start()
    w_loads = [
        pltpu.make_async_copy(w, W.at[:, pl.ds(i * cols, cols)], w_sem.at[i])
        for i, w in enumerate((wk, wv, wq))
    ]
    for load in w_loads:
        load.start()

    barrier = pltpu.get_barrier_semaphore()

    def hello(tm, head):
        pl.semaphore_signal(barrier, inc=1, device_id=(tm, head), device_id_type=MESH)

    hello(t, z_slot)
    hello(t, c_slot)
    hello(other, h)

    @pl.loop(0, PIECES)
    def _(j):
        @pl.when(j != pos)
        def _():
            hello(member(j, z_hi), h)

    far_up = jnp.logical_and(x_pos == NX - 1, t < n_tm - 1)
    far_down = jnp.logical_and(x_pos == 0, t > 0)

    @pl.when(far_up)
    def _():
        hello(up, h)

    @pl.when(far_down)
    def _():
        hello(down, h)

    pl.semaphore_wait(barrier, PIECES + 2 + far_up.astype(jnp.int32) + far_down.astype(jnp.int32))

    def halo(side, c):
        rows = pl.ds(pl.multiple_of(c * STEP, STEP), STEP)
        return pltpu.make_async_remote_copy(
            src_ref=frames.at[1 - side, rows, :],
            dst_ref=XF.at[3 * side, rows, :],
            send_sem=hs.at[side, c],
            recv_sem=hr.at[side, c],
            device_id=(down if side else up, h),
            device_id_type=MESH,
        )

    @pl.when(t > 0)
    def _():
        for c in range(chunks):
            halo(1, c).start()

    @pl.when(t < n_tm - 1)
    def _():
        for c in range(chunks):
            halo(0, c).start()

    @pl.when(is_first)
    def _():
        XF[0] = jnp.zeros((tok, ch), BF16)

    @pl.when(is_last)
    def _():
        XF[3] = jnp.zeros((tok, ch), BF16)

    def frame_of(phase):
        return jnp.where(is_first, phase, 1 - phase)

    def block(s):
        return pl.ds(pl.multiple_of(frame_of(s // chunks) * tok + lax.rem(s, chunks) * STEP, STEP), STEP)

    def remote(src, dst, send, recv, tm, head):
        return pltpu.make_async_remote_copy(
            src_ref=src, dst_ref=dst, send_sem=send, recv_sem=recv, device_id=(tm, head), device_id_type=MESH
        )

    def z_copy(s):
        ref = M.at[h, block(s), :]
        return remote(ref, ref, zs.at[s], zr.at[s], t, z_slot)

    def c_copy(s):
        ref = M.at[h, block(s), :]
        return remote(ref, ref, cs.at[s], cr.at[s], t, c_slot)

    def f_copy(s):
        ref = M.at[z_slot, block(s), :]
        return remote(ref, ref, fs.at[s], fr.at[s], t, c_slot)

    def convolve(s):
        frame = frame_of(s // chunks)
        c = lax.rem(s, chunks)

        @pl.when(s < chunks)
        def _():
            frame_load(c).wait()

        @pl.when(jnp.logical_and(frame == 1, t < n_tm - 1))
        def _():
            halo(1, c).wait_recv()

        @pl.when(jnp.logical_and(frame == 0, t > 0))
        def _():
            halo(0, c).wait_recv()

        rows_each = 32

        @pl.loop(0, STEP // rows_each)
        def _(i):
            start = pl.multiple_of(c * STEP + i * rows_each, rows_each)
            rows = pl.ds(start, rows_each)
            centre = XF[frame + 1, rows, :].astype(F32)
            before = XF[frame, rows, :].astype(F32)
            after = XF[frame + 2, rows, :].astype(F32)
            mixed = centre + taps[0:1, :] * before + taps[1:2, :] * centre + taps[2:3, :] * after
            into = pl.ds(pl.multiple_of(frame * tok + start, rows_each), rows_each)
            M[h, into, :] = mixed.astype(BF16)

        z_copy(s).start()
        c_copy(s).start()

    def scaled(raw, gain):
        mean_sq = jnp.mean(raw * raw, axis=-1, keepdims=True)
        return raw * lax.rsqrt(mean_sq + 1e-06) * gain

    def project(rows, col0, width):
        total = None
        for slot in range(4):
            term = jnp.dot(
                M[slot, rows, :], W[pl.ds(slot * ch, ch), pl.ds(col0, width)], preferred_element_type=F32
            )
            total = term if total is None else total + term
        return total

    @pl.loop(0, 2)
    def _(s):
        convolve(s)

    anchor_slot = jnp.where(is_first, 1, 3)

    def kv_copy(half):
        rows = pl.ds(pl.multiple_of(half * GROUP, GROUP), GROUP)
        return remote(KVB.at[2, rows, :], KVB.at[0, rows, :], ks.at[half], kr.at[half], up, h)

    def piece(j):
        return pl.ds(pl.multiple_of(j * piece_rows, piece_rows), piece_rows)

    def scatter_copy(j):
        return remote(KVB.at[1, piece(j), :], KVB.at[3, piece(j), :], ls.at[j], pr.at[j], member(j, 0), h)

    def fan_copy(j, tm):
        return remote(KVB.at[anchor_slot, piece(pos), :], KVB.at[3, piece(pos), :], bs.at[j], pr.at[pos], tm, h)

    def await_piece(j):
        return remote(KVB.at[3, piece(j), :], KVB.at[3, piece(j), :], ls.at[j], pr.at[j], other, h)

    def fan_out(act):
        @pl.loop(0, PIECES)
        def _(j):
            to_plane = jnp.logical_and(j != pos, jnp.logical_or(j != 0, z_hi == 1))

            @pl.when(to_plane)
            def _():
                act(fan_copy(j, member(j, z_hi)))

        @pl.when(z_hi == 0)
        def _():
            act(fan_copy(pos, other))

    @pl.loop(0, 2 * halves)
    def _(g):
        @pl.when(g < 2 * halves - 1)
        def _():
            @pl.loop(0, 2)
            def _(i):
                convolve(2 * g + 2 + i)

        @pl.loop(0, 2)
        def _(i):
            s = 2 * g + i
            z_ref = M.at[z_slot, block(s), :]
            remote(z_ref, z_ref, zs.at[s], zr.at[s], t, z_slot).wait_recv()
            f_copy(s).start()

        @pl.loop(0, 2)
        def _(i):
            s = 2 * g + i
            c_ref = M.at[c_slot, block(s), :]
            remote(c_ref, c_ref, cs.at[s], cr.at[s], t, c_slot).wait_recv()
            f_ref = M.at[f_slot, block(s), :]
            remote(f_ref, f_ref, fs.at[s], fr.at[s], t, c_slot).wait_recv()

        @pl.when(g == 0)
        def _():
            for load in w_loads:
                load.wait()

        frame = frame_of(g // halves)
        half = lax.rem(g, halves)
        m_rows = pl.ds(pl.multiple_of(frame * tok + half * GROUP, GROUP), GROUP)
        k_rows = pl.ds(pl.multiple_of(half * GROUP, GROUP), GROUP)

        @pl.loop(0, heads)
        def _(n):
            col0 = pl.multiple_of(n * 2 * DH, 2 * DH)
            raw = project(m_rows, col0, 2 * DH)
            for i in range(2):
                part = raw[:, i * DH : (i + 1) * DH]
                at = pl.ds(pl.multiple_of(col0 + i * DH, DH), DH)
                normed = scaled(part, gain_kv[:, at])
                keep = jnp.where(2 * n + i < heads, normed, part)
                KVB[frame + 1, k_rows, at] = keep.astype(BF16)

        @pl.loop(0, heads // 2)
        def _(n):
            col0 = pl.multiple_of(n * 2 * DH, 2 * DH)
            raw = project(m_rows, 2 * cols + col0, 2 * DH)
            for i in range(2):
                at = pl.ds(pl.multiple_of(col0 + i * DH, DH), DH)
                Q[m_rows, at] = scaled(raw[:, i * DH : (i + 1) * DH], gain_q[:, at]).astype(BF16)

        if heads % 2:
            at = pl.ds((heads - 1) * DH, DH)
            raw = project(m_rows, 2 * cols + (heads - 1) * DH, DH)
            Q[m_rows, at] = scaled(raw, gain_q[:, at]).astype(BF16)

        @pl.when(jnp.logical_and(frame == 1, t < n_tm - 1))
        def _():
            kv_copy(half).start()

        @pl.when(jnp.logical_and(frame == 0, is_first))
        def _():
            each = PIECES // halves

            @pl.loop(0, each)
            def _(i):
                j = half * each + i

                @pl.when(j > 0)
                def _():
                    scatter_copy(j).start()

        @pl.when(jnp.logical_and(g == 1, z_hi == 0))
        def _():
            @pl.when(t > 0)
            def _():
                await_piece(pos).wait_recv()

            fan_out(lambda copy: copy.start())

        @pl.when(jnp.logical_and(g == 2, z_hi == 1))
        def _():
            await_piece(pos).wait_recv()
            fan_out(lambda copy: copy.start())

    @pl.when(t > 0)
    def _():
        @pl.loop(0, PIECES)
        def _(j):
            @pl.when(j != pos)
            def _():
                await_piece(j).wait_recv()

    factor = math.log2(math.e) / DH**0.5

    def attend(frame, prev_slot):
        @pl.loop(0, heads * halves)
        def _(i):
            head = i // halves
            block_q = lax.rem(i, halves)
            k_at = pl.ds(pl.multiple_of(head * DH, DH), DH)
            v_at = pl.ds(pl.multiple_of(cols + head * DH, DH), DH)
            q = Q[pl.ds(pl.multiple_of(frame * tok + block_q * GROUP, GROUP), GROUP), k_at]
            dims = (((1,), (1,)), ((), ()))
            s0 = lax.dot_general(q, KVB[anchor_slot, :, k_at], dims, preferred_element_type=F32)
            s1 = lax.dot_general(q, KVB[prev_slot, :, k_at], dims, preferred_element_type=F32)
            top = jnp.maximum(jnp.max(s0, axis=-1, keepdims=True), jnp.max(s1, axis=-1, keepdims=True))
            e0 = jnp.exp2((s0 - top) * factor)
            e1 = jnp.exp2((s1 - top) * factor)
            norm = jnp.sum(e0, axis=-1, keepdims=True) + jnp.sum(e1, axis=-1, keepdims=True)
            acc = jnp.dot(e0.astype(BF16), KVB[anchor_slot, :, v_at], preferred_element_type=F32)
            acc += jnp.dot(e1.astype(BF16), KVB[prev_slot, :, v_at], preferred_element_type=F32)
            out[frame, pl.ds(pl.multiple_of(block_q * GROUP, GROUP), GROUP), k_at] = (acc / norm).astype(BF16)

    attend(1, 1)

    @pl.when(t > 0)
    def _():
        for half in range(halves):
            kv_copy(half).wait_recv()

    attend(0, jnp.where(is_first, 1, 0))

    @pl.loop(0, 2 * chunks)
    def _(s):
        z_copy(s).wait_send()
        c_copy(s).wait_send()
        f_copy(s).wait_send()

    @pl.when(t > 0)
    def _():
        for c in range(chunks):
            halo(1, c).wait_send()

    @pl.when(t < n_tm - 1)
    def _():
        for c in range(chunks):
            halo(0, c).wait_send()
        for half in range(halves):
            kv_copy(half).wait_send()

    @pl.when(is_first)
    def _():
        @pl.loop(1, PIECES)
        def _(j):
            scatter_copy(j).wait_send()

    fan_out(lambda copy: copy.wait_send())


def per_device(frames, taps, w_query, w_key, w_value, q_gain, k_gain):
    count, tok, ch = frames.shape
    depth, cols = w_query.shape
    chunks = tok // STEP
    halves = tok // GROUP
    gain_kv = jnp.concatenate([k_gain, jnp.ones_like(k_gain)])[None]
    gain_q = q_gain[None]
    dma = pltpu.SemaphoreType.DMA
    vmem = pl.BlockSpec(memory_space=pltpu.VMEM)
    anywhere = pl.BlockSpec(memory_space=pl.ANY)
    return pl.pallas_call(
        kernel,
        out_shape=jax.ShapeDtypeStruct((count, tok, cols), BF16),
        in_specs=[anywhere, vmem, vmem, vmem, anywhere, anywhere, anywhere],
        out_specs=vmem,
        scratch_shapes=[
            pltpu.VMEM((4, tok, ch), BF16),
            pltpu.VMEM((4, count * tok, ch), BF16),
            pltpu.VMEM((depth, 3 * cols), BF16),
            pltpu.VMEM((4, tok, 2 * cols), BF16),
            pltpu.VMEM((count * tok, cols), BF16),
            dma((3,)),
            dma((chunks,)),
            dma((2, chunks)),
            dma((2, chunks)),
            dma((2 * chunks,)),
            dma((2 * chunks,)),
            dma((2 * chunks,)),
            dma((2 * chunks,)),
            dma((2 * chunks,)),
            dma((2 * chunks,)),
            dma((halves,)),
            dma((halves,)),
            dma((PIECES,)),
            dma((PIECES,)),
            dma((PIECES,)),
        ],
        compiler_params=pltpu.CompilerParams(
            collective_id=0, has_side_effects=True, vmem_limit_bytes=62 * 1024 * 1024
        ),
    )(frames, taps, gain_kv, gain_q, w_query, w_key, w_value)


def solution(mesh):
    placed = (
        P("tm", None, "head"),
        P(None, "head"),
        P(None, "head"),
        P(None, "head"),
        P(None, "head"),
        P("head"),
        P("head"),
    )
    return jax.shard_map(
        per_device, mesh=mesh, in_specs=placed, out_specs=P("tm", None, "head"), check_vma=False
    )
```

time: 619 us -> 162 us (0.26)
  the two profiles are of different devices: /device:TPU:0 before, /device:TPU:3 now
where the time goes in v1:
time: 162 us
  Pallas kernels  157 us (97%)
  local copies, waits for them, and re-layouts  5.04 us (3%)
    pallas_call x1, Pallas kernels, per_device(): pl.pallas_call(kernel, out_shape=jax.ShapeDtypeStruct((count, tok, cols),...  157 us

profile of v1, /device:TPU:3, one launch (start us, length us, event | category | flops | bytes accessed | tf_op | source)
XLA Modules:
  0.0 161.7 jit_solution(13094607024336743445)
XLA Ops:
  0.0 1.3 broadcast_in_dim.8.gain_q
  1.3 0.7 concatenate.3
  2.0 0.6 broadcast_in_dim.7.gain_kv
  2.6 156.6 %shard_map.73 = bf16[2,512,640]{2,1,0:T(8,128)(2,1)} custom-call(bf16[2,512,1280]{2,1,0:T(8,128)(2,1)} %frames.1, f32[3,1280]{1,0:T(4,128)} %taps.1, f32[1,1280]{1,0:T(1,128)} %broadcast_in_dim.7.gain_kv, f32[1,640]{1,0:T(1,128)} %broadcast_in_dim.8.gain_q, bf16[5120,640]{1,0:T(8,128)(2,1)} %wq.1, bf16[5120,640]{1,0:T(8,128)(2,1)} %wk.1, bf16[5120,640]{1,0:T(8,128)(2,1)} %wv.1), custom_call_target="tpu_custom_call" | custom-call | tf_op jit(solution)/shard_map/pallas_call | solution.py:385
  159.2 2.5 %copy.9 = bf16[2,512,640]{2,1,0:T(8,128)(2,1)} copy(bf16[2,512,640]{2,1,0:T(8,128)(2,1)} %shard_map.73) | data formatting | bytes 2621440

commit v2 on v1

--- a/solution.py
+++ b/solution.py
@@ -20,8 +20,8 @@
 GROUP = 256
 
 
-def kernel(frames, taps, gain_kv, gain_q, wq, wk, wv, out, XF, M, W, KVB, Q,
-           w_sem, f_sem, hs, hr, zs, zr, cs, cr, fs, fr, ks, kr, ls, bs, pr):
+def kernel(frames, taps, gain_kv, gain_q, wq, wk, wv, out, XF, M, W, KVB, Q, KVR,
+           w_sem, f_sem, hs, hr, zs, zr, cs, cr, fs, fr, ks, kr, rs, rr, ls, bs, pr):
     n_tm = lax.axis_size("tm")
     t = lax.axis_index("tm")
     h = lax.axis_index("head")
@@ -43,7 +43,8 @@
     z_slot = lax.rem(h + 2, 4)
     c_slot = h + 1 - 2 * lax.rem(h, 2)
     f_slot = lax.rem(c_slot + 2, 4)
-    other = t + NX - 2 * NX * z_hi
+    row = t // NX
+    n_rows = n_tm // NX
 
     def member(j, plane):
         return (j // NX) * ROW + plane * NX + lax.rem(j, NX)
@@ -68,7 +69,6 @@
 
     hello(t, z_slot)
     hello(t, c_slot)
-    hello(other, h)
 
     @pl.loop(0, PIECES)
     def _(j):
@@ -76,18 +76,35 @@
         def _():
             hello(member(j, z_hi), h)
 
-    far_up = jnp.logical_and(x_pos == NX - 1, t < n_tm - 1)
-    far_down = jnp.logical_and(x_pos == 0, t > 0)
-
-    @pl.when(far_up)
-    def _():
-        hello(up, h)
-
-    @pl.when(far_down)
+        @pl.when(is_first)
+        def _():
+            hello(member(j, 1), h)
+
+    has_next = jnp.logical_and(x_pos == NX - 1, t < n_tm - 1)
+    has_prev = jnp.logical_and(x_pos == 0, t > 0)
+    is_relay = jnp.logical_and(jnp.logical_and(x_pos > 0, x_pos < NX - 1), row > 0)
+
+    @pl.when(has_next)
+    def _():
+        for i in range(1, NX):
+            hello(t + i, h)
+
+    @pl.when(has_prev)
     def _():
         hello(down, h)
 
-    pl.semaphore_wait(barrier, PIECES + 2 + far_up.astype(jnp.int32) + far_down.astype(jnp.int32))
+    @pl.when(is_relay)
+    def _():
+        hello(row * NX - 1, h)
+
+    @pl.when(z_hi == 1)
+    def _():
+        hello(0, h)
+
+    expected = PIECES + 1 + z_hi
+    for cond, count in ((has_next, NX - 1), (has_prev, 1), (is_relay, 1), (is_first, PIECES)):
+        expected = expected + jnp.where(cond, count, 0)
+    pl.semaphore_wait(barrier, expected)
 
     def halo(side, c):
         rows = pl.ds(pl.multiple_of(c * STEP, STEP), STEP)
@@ -192,67 +209,65 @@
 
     anchor_slot = jnp.where(is_first, 1, 3)
 
+    def half_rows(half):
+        return pl.ds(pl.multiple_of(half * GROUP, GROUP), GROUP)
+
     def kv_copy(half):
-        rows = pl.ds(pl.multiple_of(half * GROUP, GROUP), GROUP)
+        rows = half_rows(half)
         return remote(KVB.at[2, rows, :], KVB.at[0, rows, :], ks.at[half], kr.at[half], up, h)
+
+    def relay_in(half):
+        return remote(KVB.at[2, half_rows(half), :], KVR, ks.at[half], rr.at[0], lax.rem(t + 2 + half, n_tm), h)
+
+    def relay_out(half):
+        return remote(KVR, KVB.at[0, half_rows(half), :], rs.at[0], kr.at[half], row * NX, h)
+
+    def send_kv(half, act):
+        @pl.when(has_next)
+        def _():
+            act(relay_in(half))
+
+        @pl.when(x_pos < NX - 1)
+        def _():
+            act(kv_copy(half))
 
     def piece(j):
         return pl.ds(pl.multiple_of(j * piece_rows, piece_rows), piece_rows)
 
-    def scatter_copy(j):
-        return remote(KVB.at[1, piece(j), :], KVB.at[3, piece(j), :], ls.at[j], pr.at[j], member(j, 0), h)
-
-    def fan_copy(j, tm):
-        return remote(KVB.at[anchor_slot, piece(pos), :], KVB.at[3, piece(pos), :], bs.at[j], pr.at[pos], tm, h)
+    def scatter_copy(j, plane):
+        return remote(KVB.at[1, piece(j), :], KVB.at[3, piece(j), :], ls.at[plane, j], pr.at[j], member(j, plane), h)
+
+    def fan_copy(j):
+        return remote(
+            KVB.at[anchor_slot, piece(pos), :], KVB.at[3, piece(pos), :], bs.at[j], pr.at[pos], member(j, z_hi), h
+        )
 
     def await_piece(j):
-        return remote(KVB.at[3, piece(j), :], KVB.at[3, piece(j), :], ls.at[j], pr.at[j], other, h)
+        return remote(KVB.at[3, piece(j), :], KVB.at[3, piece(j), :], ls.at[0, j], pr.at[j], member(j, 1 - z_hi), h)
 
     def fan_out(act):
         @pl.loop(0, PIECES)
         def _(j):
-            to_plane = jnp.logical_and(j != pos, jnp.logical_or(j != 0, z_hi == 1))
-
-            @pl.when(to_plane)
+            @pl.when(jnp.logical_and(j != pos, jnp.logical_or(j != 0, z_hi == 1)))
             def _():
-                act(fan_copy(j, member(j, z_hi)))
-
-        @pl.when(z_hi == 0)
-        def _():
-            act(fan_copy(pos, other))
-
-    @pl.loop(0, 2 * halves)
-    def _(g):
-        @pl.when(g < 2 * halves - 1)
-        def _():
-            @pl.loop(0, 2)
-            def _(i):
-                convolve(2 * g + 2 + i)
-
-        @pl.loop(0, 2)
-        def _(i):
-            s = 2 * g + i
-            z_ref = M.at[z_slot, block(s), :]
-            remote(z_ref, z_ref, zs.at[s], zr.at[s], t, z_slot).wait_recv()
-            f_copy(s).start()
-
-        @pl.loop(0, 2)
-        def _(i):
-            s = 2 * g + i
-            c_ref = M.at[c_slot, block(s), :]
-            remote(c_ref, c_ref, cs.at[s], cr.at[s], t, c_slot).wait_recv()
-            f_ref = M.at[f_slot, block(s), :]
-            remote(f_ref, f_ref, fs.at[s], fr.at[s], t, c_slot).wait_recv()
-
-        @pl.when(g == 0)
-        def _():
-            for load in w_loads:
-                load.wait()
-
-        frame = frame_of(g // halves)
-        half = lax.rem(g, halves)
-        m_rows = pl.ds(pl.multiple_of(frame * tok + half * GROUP, GROUP), GROUP)
-        k_rows = pl.ds(pl.multiple_of(half * GROUP, GROUP), GROUP)
+                act(fan_copy(j))
+
+    each = PIECES // halves
+
+    def scatter(half, act):
+        @pl.loop(0, each)
+        def _(i):
+            j = half * each + i
+
+            @pl.when(j > 0)
+            def _():
+                act(scatter_copy(j, 0))
+
+            act(scatter_copy(j, 1))
+
+    def qkv(frame, first, count):
+        m_rows = pl.ds(pl.multiple_of(frame * tok + first, count), count)
+        k_rows = pl.ds(pl.multiple_of(first, count), count)
 
         @pl.loop(0, heads)
         def _(n):
@@ -278,23 +293,56 @@
             raw = project(m_rows, 2 * cols + (heads - 1) * DH, DH)
             Q[m_rows, at] = scaled(raw, gain_q[:, at]).astype(BF16)
 
+    def forward(s):
+        z_ref = M.at[z_slot, block(s), :]
+        remote(z_ref, z_ref, zs.at[s], zr.at[s], t, z_slot).wait_recv()
+        f_copy(s).start()
+
+    def gathered(s):
+        c_ref = M.at[c_slot, block(s), :]
+        remote(c_ref, c_ref, cs.at[s], cr.at[s], t, c_slot).wait_recv()
+        f_ref = M.at[f_slot, block(s), :]
+        remote(f_ref, f_ref, fs.at[s], fr.at[s], t, c_slot).wait_recv()
+
+    groups = 2 * halves
+
+    @pl.loop(0, groups - 1)
+    def _(g):
+        @pl.loop(0, 2)
+        def _(i):
+            convolve(2 * g + 2 + i)
+
+        @pl.loop(0, 2)
+        def _(i):
+            forward(2 * g + i)
+
+        @pl.loop(0, 2)
+        def _(i):
+            gathered(2 * g + i)
+
+        @pl.when(g == 0)
+        def _():
+            for load in w_loads:
+                load.wait()
+
+        frame = frame_of(g // halves)
+        half = lax.rem(g, halves)
+        qkv(frame, half * GROUP, GROUP)
+
         @pl.when(jnp.logical_and(frame == 1, t < n_tm - 1))
         def _():
-            kv_copy(half).start()
+            send_kv(half, lambda copy: copy.start())
 
         @pl.when(jnp.logical_and(frame == 0, is_first))
         def _():
-            each = PIECES // halves
-
-            @pl.loop(0, each)
-            def _(i):
-                j = half * each + i
-
-                @pl.when(j > 0)
-                def _():
-                    scatter_copy(j).start()
-
-        @pl.when(jnp.logical_and(g == 1, z_hi == 0))
+            scatter(half, lambda copy: copy.start())
+
+        @pl.when(jnp.logical_and(is_relay, g == x_pos))
+        def _():
+            relay_in(x_pos - 1).wait_recv()
+            relay_out(x_pos - 1).start()
+
+        @pl.when(g == 1 + pos // each)
         def _():
             @pl.when(t > 0)
             def _():
@@ -302,10 +350,15 @@
 
             fan_out(lambda copy: copy.start())
 
-        @pl.when(jnp.logical_and(g == 2, z_hi == 1))
-        def _():
-            await_piece(pos).wait_recv()
-            fan_out(lambda copy: copy.start())
+    @pl.loop(2 * groups - 2, 2 * groups)
+    def _(s):
+        forward(s)
+        gathered(s)
+        qkv(frame_of(1), lax.rem(s, chunks) * STEP, STEP)
+
+    @pl.when(is_first)
+    def _():
+        send_kv(halves - 1, lambda copy: copy.start())
 
     @pl.when(t > 0)
     def _():
@@ -361,13 +414,16 @@
         for c in range(chunks):
             halo(0, c).wait_send()
         for half in range(halves):
-            kv_copy(half).wait_send()
+            send_kv(half, lambda copy: copy.wait_send())
+
+    @pl.when(is_relay)
+    def _():
+        relay_out(x_pos - 1).wait_send()
 
     @pl.when(is_first)
     def _():
-        @pl.loop(1, PIECES)
-        def _(j):
-            scatter_copy(j).wait_send()
+        for half in range(halves):
+            scatter(half, lambda copy: copy.wait_send())
 
     fan_out(lambda copy: copy.wait_send())
 
@@ -393,6 +449,7 @@
             pltpu.VMEM((depth, 3 * cols), BF16),
             pltpu.VMEM((4, tok, 2 * cols), BF16),
             pltpu.VMEM((count * tok, cols), BF16),
+            pltpu.VMEM((GROUP, 2 * cols), BF16),
             dma((3,)),
             dma((chunks,)),
             dma((2, chunks)),
@@ -405,7 +462,9 @@
             dma((2 * chunks,)),
             dma((halves,)),
             dma((halves,)),
-            dma((PIECES,)),
+            dma((1,)),
+            dma((1,)),
+            dma((2, PIECES)),
             dma((PIECES,)),
             dma((PIECES,)),
         ],

time: 162 us -> 154 us (0.951)
  Pallas kernels: 157 us -> 149 us
    pallas_call x1, Pallas kernels: 157 us -> 149 us  [per_device(): pl.pallas_call(kernel, out_shape=jax.ShapeDtypeStruct((count, tok, cols),...]
where the time goes in v2:
time: 154 us
  Pallas kernels  149 us (97%)
  local copies, waits for them, and re-layouts  5.04 us (3%)
    pallas_call x1, Pallas kernels, per_device(): pl.pallas_call(kernel, out_shape=jax.ShapeDtypeStruct((count, tok, cols),...  149 us

profile of v2, /device:TPU:3, one launch (start us, length us, event | category | flops | bytes accessed | tf_op | source)
XLA Modules:
  0.0 153.8 jit_solution(9514565354520618911)
XLA Ops:
  0.0 1.3 broadcast_in_dim.8.gain_q
  1.3 0.7 concatenate.3
  2.0 0.6 broadcast_in_dim.7.gain_kv
  2.6 148.8 %shard_map.73 = bf16[2,512,640]{2,1,0:T(8,128)(2,1)} custom-call(bf16[2,512,1280]{2,1,0:T(8,128)(2,1)} %frames.1, f32[3,1280]{1,0:T(4,128)} %taps.1, f32[1,1280]{1,0:T(1,128)} %broadcast_in_dim.7.gain_kv, f32[1,640]{1,0:T(1,128)} %broadcast_in_dim.8.gain_q, bf16[5120,640]{1,0:T(8,128)(2,1)} %wq.1, bf16[5120,640]{1,0:T(8,128)(2,1)} %wk.1, bf16[5120,640]{1,0:T(8,128)(2,1)} %wv.1), custom_call_target="tpu_custom_call" | custom-call | tf_op jit(solution)/shard_map/pallas_call | solution.py:441
  151.3 2.5 %copy.9 = bf16[2,512,640]{2,1,0:T(8,128)(2,1)} copy(bf16[2,512,640]{2,1,0:T(8,128)(2,1)} %shard_map.73) | data formatting | bytes 2621440

commit v3 on v2

--- a/solution.py
+++ b/solution.py
@@ -20,8 +20,8 @@
 GROUP = 256
 
 
-def kernel(frames, taps, gain_kv, gain_q, wq, wk, wv, out, XF, M, W, KVB, Q, KVR,
-           w_sem, f_sem, hs, hr, zs, zr, cs, cr, fs, fr, ks, kr, rs, rr, ls, bs, pr):
+def kernel(frames, taps, gain_q, gain_k, wq, wk, wv, out, XF, M, W, KVB, Q, KVR, HR,
+           w_sem, f_sem, hs, hr, zs, zr, cs, cr, fs, fr, ks, kr, rs, rr, us, ur, ls, bs, pr):
     n_tm = lax.axis_size("tm")
     t = lax.axis_index("tm")
     h = lax.axis_index("head")
@@ -82,69 +82,106 @@
 
     has_next = jnp.logical_and(x_pos == NX - 1, t < n_tm - 1)
     has_prev = jnp.logical_and(x_pos == 0, t > 0)
-    is_relay = jnp.logical_and(jnp.logical_and(x_pos > 0, x_pos < NX - 1), row > 0)
+    inner = jnp.logical_and(x_pos > 0, x_pos < NX - 1)
+    kv_relay = jnp.logical_and(inner, row > 0)
+    down_relay = jnp.logical_and(inner, row < n_rows - 1)
+    up_relay = jnp.logical_and(x_pos == NX - 1, row > 0)
 
     @pl.when(has_next)
     def _():
+        for i in range(1, NX + 1):
+            hello(t + i, h)
+
+    @pl.when(has_prev)
+    def _():
         for i in range(1, NX):
-            hello(t + i, h)
-
-    @pl.when(has_prev)
-    def _():
-        hello(down, h)
-
-    @pl.when(is_relay)
+            hello(t - i, h)
+
+    @pl.when(jnp.logical_or(kv_relay, up_relay))
     def _():
         hello(row * NX - 1, h)
 
+    @pl.when(down_relay)
+    def _():
+        hello(row * NX + NX, h)
+
     @pl.when(z_hi == 1)
     def _():
         hello(0, h)
 
     expected = PIECES + 1 + z_hi
-    for cond, count in ((has_next, NX - 1), (has_prev, 1), (is_relay, 1), (is_first, PIECES)):
+    for cond, count in (
+        (has_next, NX),
+        (has_prev, NX - 1),
+        (kv_relay, 1),
+        (up_relay, 1),
+        (down_relay, 1),
+        (is_first, PIECES),
+    ):
         expected = expected + jnp.where(cond, count, 0)
     pl.semaphore_wait(barrier, expected)
-
-    def halo(side, c):
-        rows = pl.ds(pl.multiple_of(c * STEP, STEP), STEP)
-        return pltpu.make_async_remote_copy(
-            src_ref=frames.at[1 - side, rows, :],
-            dst_ref=XF.at[3 * side, rows, :],
-            send_sem=hs.at[side, c],
-            recv_sem=hr.at[side, c],
-            device_id=(down if side else up, h),
-            device_id_type=MESH,
-        )
-
-    @pl.when(t > 0)
-    def _():
-        for c in range(chunks):
-            halo(1, c).start()
-
-    @pl.when(t < n_tm - 1)
-    def _():
-        for c in range(chunks):
-            halo(0, c).start()
-
-    @pl.when(is_first)
-    def _():
-        XF[0] = jnp.zeros((tok, ch), BF16)
-
-    @pl.when(is_last)
-    def _():
-        XF[3] = jnp.zeros((tok, ch), BF16)
-
-    def frame_of(phase):
-        return jnp.where(is_first, phase, 1 - phase)
-
-    def block(s):
-        return pl.ds(pl.multiple_of(frame_of(s // chunks) * tok + lax.rem(s, chunks) * STEP, STEP), STEP)
 
     def remote(src, dst, send, recv, tm, head):
         return pltpu.make_async_remote_copy(
             src_ref=src, dst_ref=dst, send_sem=send, recv_sem=recv, device_id=(tm, head), device_id_type=MESH
         )
+
+    def step_rows(c):
+        return pl.ds(pl.multiple_of(c * STEP, STEP), STEP)
+
+    def halo(side, c):
+        rows = step_rows(c)
+        to = down if side else up
+        return remote(frames.at[1 - side, rows, :], XF.at[3 * side, rows, :], hs.at[side, c], hr.at[side, c], to, h)
+
+    def halo_in(side, c):
+        to = lax.rem(t + NX, n_tm) if side == 0 else lax.rem(t - c + n_tm, n_tm)
+        return remote(frames.at[1 - side, step_rows(c), :], HR, hs.at[side, c], ur.at[0], to, h)
+
+    def halo_sends(act):
+        for c in range(chunks):
+            for side, some, far in ((1, t > 0, x_pos == 0), (0, t < n_tm - 1, x_pos == NX - 1)):
+                relayed = c >= chunks - (2 if side else 1)
+
+                if relayed:
+                    @pl.when(jnp.logical_and(some, far))
+                    def _():
+                        act(halo_in(side, c))
+
+                    @pl.when(jnp.logical_and(some, jnp.logical_not(far)))
+                    def _():
+                        act(halo(side, c))
+                else:
+                    @pl.when(some)
+                    def _():
+                        act(halo(side, c))
+
+    halo_sends(lambda copy: copy.start())
+
+    def down_out():
+        c = chunks - x_pos
+        return remote(HR, XF.at[3, step_rows(c), :], us.at[0], hr.at[1, c], row * NX + NX - 1, h)
+
+    def up_out():
+        c = chunks - 1
+        return remote(HR, XF.at[0, step_rows(c), :], us.at[0], hr.at[0, c], row * NX, h)
+
+    def halo_arrived():
+        halo_in(0, chunks - 1).wait_recv()
+
+    @pl.when(is_first)
+    def _():
+        XF[0] = jnp.zeros((tok, ch), BF16)
+
+    @pl.when(is_last)
+    def _():
+        XF[3] = jnp.zeros((tok, ch), BF16)
+
+    def frame_of(phase):
+        return jnp.where(is_first, phase, 1 - phase)
+
+    def block(s):
+        return pl.ds(pl.multiple_of(frame_of(s // chunks) * tok + lax.rem(s, chunks) * STEP, STEP), STEP)
 
     def z_copy(s):
         ref = M.at[h, block(s), :]
@@ -209,27 +246,32 @@
 
     anchor_slot = jnp.where(is_first, 1, 3)
 
-    def half_rows(half):
-        return pl.ds(pl.multiple_of(half * GROUP, GROUP), GROUP)
-
-    def kv_copy(half):
-        rows = half_rows(half)
-        return remote(KVB.at[2, rows, :], KVB.at[0, rows, :], ks.at[half], kr.at[half], up, h)
-
-    def relay_in(half):
-        return remote(KVB.at[2, half_rows(half), :], KVR, ks.at[half], rr.at[0], lax.rem(t + 2 + half, n_tm), h)
+    def kv_copy(c):
+        rows = step_rows(c)
+        return remote(KVB.at[2, rows, :], KVB.at[0, rows, :], ks.at[c], kr.at[c], up, h)
+
+    def relay_in(c):
+        to = lax.rem(t + 2 + lax.rem(c, 2), n_tm)
+        return remote(KVB.at[2, step_rows(c), :], KVR.at[c // 2], ks.at[c], rr.at[c // 2], to, h)
 
     def relay_out(half):
-        return remote(KVR, KVB.at[0, half_rows(half), :], rs.at[0], kr.at[half], row * NX, h)
-
-    def send_kv(half, act):
+        c = 2 * half + x_pos - 1
+        return remote(KVR.at[half], KVB.at[0, step_rows(c), :], rs.at[half], kr.at[c], row * NX, h)
+
+    def send_kv(c, act):
         @pl.when(has_next)
         def _():
-            act(relay_in(half))
+            act(relay_in(c))
 
         @pl.when(x_pos < NX - 1)
         def _():
-            act(kv_copy(half))
+            act(kv_copy(c))
+
+    def pass_kv(half):
+        @pl.when(kv_relay)
+        def _():
+            relay_in(2 * half).wait_recv()
+            relay_out(half).start()
 
     def piece(j):
         return pl.ds(pl.multiple_of(j * piece_rows, piece_rows), piece_rows)
@@ -276,8 +318,9 @@
             for i in range(2):
                 part = raw[:, i * DH : (i + 1) * DH]
                 at = pl.ds(pl.multiple_of(col0 + i * DH, DH), DH)
-                normed = scaled(part, gain_kv[:, at])
-                keep = jnp.where(2 * n + i < heads, normed, part)
+                is_key = 2 * n + i < heads
+                at_k = pl.ds(pl.multiple_of(jnp.where(is_key, col0 + i * DH, 0), DH), DH)
+                keep = jnp.where(is_key, scaled(part, gain_k[at_k]), part)
                 KVB[frame + 1, k_rows, at] = keep.astype(BF16)
 
         @pl.loop(0, heads // 2)
@@ -286,12 +329,12 @@
             raw = project(m_rows, 2 * cols + col0, 2 * DH)
             for i in range(2):
                 at = pl.ds(pl.multiple_of(col0 + i * DH, DH), DH)
-                Q[m_rows, at] = scaled(raw[:, i * DH : (i + 1) * DH], gain_q[:, at]).astype(BF16)
+                Q[m_rows, at] = scaled(raw[:, i * DH : (i + 1) * DH], gain_q[at]).astype(BF16)
 
         if heads % 2:
             at = pl.ds((heads - 1) * DH, DH)
             raw = project(m_rows, 2 * cols + (heads - 1) * DH, DH)
-            Q[m_rows, at] = scaled(raw, gain_q[:, at]).astype(BF16)
+            Q[m_rows, at] = scaled(raw, gain_q[at]).astype(BF16)
 
     def forward(s):
         z_ref = M.at[z_slot, block(s), :]
@@ -306,11 +349,14 @@
 
     groups = 2 * halves
 
+    @pl.when(down_relay)
+    def _():
+        halo_arrived()
+        down_out().start()
+
     @pl.loop(0, groups - 1)
     def _(g):
-        @pl.loop(0, 2)
-        def _(i):
-            convolve(2 * g + 2 + i)
+        convolve(2 * g + 2)
 
         @pl.loop(0, 2)
         def _(i):
@@ -320,10 +366,29 @@
         def _(i):
             gathered(2 * g + i)
 
+        convolve(2 * g + 3)
+
         @pl.when(g == 0)
         def _():
             for load in w_loads:
                 load.wait()
+
+            @pl.when(up_relay)
+            def _():
+                halo_arrived()
+                up_out().start()
+
+        @pl.when(g == 1 + pos // each)
+        def _():
+            @pl.when(t > 0)
+            def _():
+                await_piece(pos).wait_recv()
+
+            fan_out(lambda copy: copy.start())
+
+        @pl.when(g == 2)
+        def _():
+            pass_kv(0)
 
         frame = frame_of(g // halves)
         half = lax.rem(g, halves)
@@ -331,34 +396,28 @@
 
         @pl.when(jnp.logical_and(frame == 1, t < n_tm - 1))
         def _():
-            send_kv(half, lambda copy: copy.start())
+            send_kv(2 * half, lambda copy: copy.start())
+            send_kv(2 * half + 1, lambda copy: copy.start())
 
         @pl.when(jnp.logical_and(frame == 0, is_first))
         def _():
             scatter(half, lambda copy: copy.start())
-
-        @pl.when(jnp.logical_and(is_relay, g == x_pos))
-        def _():
-            relay_in(x_pos - 1).wait_recv()
-            relay_out(x_pos - 1).start()
-
-        @pl.when(g == 1 + pos // each)
-        def _():
-            @pl.when(t > 0)
-            def _():
-                await_piece(pos).wait_recv()
-
-            fan_out(lambda copy: copy.start())
 
     @pl.loop(2 * groups - 2, 2 * groups)
     def _(s):
         forward(s)
         gathered(s)
-        qkv(frame_of(1), lax.rem(s, chunks) * STEP, STEP)
-
-    @pl.when(is_first)
-    def _():
-        send_kv(halves - 1, lambda copy: copy.start())
+
+        @pl.when(s == 2 * groups - 2)
+        def _():
+            pass_kv(1)
+
+        c = lax.rem(s, chunks)
+        qkv(frame_of(1), c * STEP, STEP)
+
+        @pl.when(is_first)
+        def _():
+            kv_copy(c).start()
 
     @pl.when(t > 0)
     def _():
@@ -393,8 +452,8 @@
 
     @pl.when(t > 0)
     def _():
-        for half in range(halves):
-            kv_copy(half).wait_recv()
+        for c in range(chunks):
+            kv_copy(c).wait_recv()
 
     attend(0, jnp.where(is_first, 1, 0))
 
@@ -404,21 +463,21 @@
         c_copy(s).wait_send()
         f_copy(s).wait_send()
 
-    @pl.when(t > 0)
+    halo_sends(lambda copy: copy.wait_send())
+
+    @pl.when(jnp.logical_or(down_relay, up_relay))
+    def _():
+        up_out().wait_send()
+
+    @pl.when(t < n_tm - 1)
     def _():
         for c in range(chunks):
-            halo(1, c).wait_send()
-
-    @pl.when(t < n_tm - 1)
-    def _():
-        for c in range(chunks):
-            halo(0, c).wait_send()
+            send_kv(c, lambda copy: copy.wait_send())
+
+    @pl.when(kv_relay)
+    def _():
         for half in range(halves):
-            send_kv(half, lambda copy: copy.wait_send())
-
-    @pl.when(is_relay)
-    def _():
-        relay_out(x_pos - 1).wait_send()
+            relay_out(half).wait_send()
 
     @pl.when(is_first)
     def _():
@@ -433,8 +492,6 @@
     depth, cols = w_query.shape
     chunks = tok // STEP
     halves = tok // GROUP
-    gain_kv = jnp.concatenate([k_gain, jnp.ones_like(k_gain)])[None]
-    gain_q = q_gain[None]
     dma = pltpu.SemaphoreType.DMA
     vmem = pl.BlockSpec(memory_space=pltpu.VMEM)
     anywhere = pl.BlockSpec(memory_space=pl.ANY)
@@ -449,7 +506,8 @@
             pltpu.VMEM((depth, 3 * cols), BF16),
             pltpu.VMEM((4, tok, 2 * cols), BF16),
             pltpu.VMEM((count * tok, cols), BF16),
-            pltpu.VMEM((GROUP, 2 * cols), BF16),
+            pltpu.VMEM((halves, STEP, 2 * cols), BF16),
+            pltpu.VMEM((STEP, ch), BF16),
             dma((3,)),
             dma((chunks,)),
             dma((2, chunks)),
@@ -460,6 +518,8 @@
             dma((2 * chunks,)),
             dma((2 * chunks,)),
             dma((2 * chunks,)),
+            dma((chunks,)),
+            dma((chunks,)),
             dma((halves,)),
             dma((halves,)),
             dma((1,)),
@@ -471,7 +531,7 @@
         compiler_params=pltpu.CompilerParams(
             collective_id=0, has_side_effects=True, vmem_limit_bytes=62 * 1024 * 1024
         ),
-    )(frames, taps, gain_kv, gain_q, w_query, w_key, w_value)
+    )(frames, taps, q_gain, k_gain, w_query, w_key, w_value)
 
 
 def solution(mesh):

time: 154 us -> 143 us (0.929); the launches traced: 154 us -> 140 us
  Pallas kernels: 149 us -> 138 us
  local copies, waits for them, and re-layouts: 5.04 us -> 2.49 us
    pallas_call x1, Pallas kernels: 149 us -> 138 us  [per_device(): pl.pallas_call(kernel, out_shape=jax.ShapeDtypeStruct((count, tok, cols),...]
    broadcast_in_dim x2 -> x0, local copies, waits for them, and re-layouts: 1.86 us -> none  [the longest x1 1.26 us: per_device(): gain_q = q_gain[None]]
where the time goes in v3:
time: 143 us; the launch traced here: 140 us
  Pallas kernels  138 us (97%)
  local copies, waits for them, and re-layouts  2.49 us (2%)
    pallas_call x1, Pallas kernels, per_device(): pl.pallas_call(kernel, out_shape=jax.ShapeDtypeStruct((count, tok, cols),...  138 us

profile of v3, /device:TPU:3, one launch (start us, length us, event | category | flops | bytes accessed | tf_op | source)
XLA Modules:
  0.0 140.3 jit_solution(5681603394361737332)
XLA Ops:
  0.0 137.8 %shard_map.73 = bf16[2,512,640]{2,1,0:T(8,128)(2,1)} custom-call(bf16[2,512,1280]{2,1,0:T(8,128)(2,1)} %frames.1, f32[3,1280]{1,0:T(4,128)} %taps.1, f32[640]{0:T(1024)} %gain_q.1, f32[640]{0:T(1024)} %gain_k.1, bf16[5120,640]{1,0:T(8,128)(2,1)} %wq.1, bf16[5120,640]{1,0:T(8,128)(2,1)} %wk.1, bf16[5120,640]{1,0:T(8,128)(2,1)} %wv.1), custom_call_target="tpu_custom_call" | custom-call | tf_op jit(solution)/shard_map/pallas_call | solution.py:498
  137.8 2.5 %copy.9 = bf16[2,512,640]{2,1,0:T(8,128)(2,1)} copy(bf16[2,512,640]{2,1,0:T(8,128)(2,1)} %shard_map.73) | data formatting | bytes 2621440
